TPU v7x, 256 devices: a whole 4x4x8 slice. The times are simulated.
256 devices in a mesh: role: 2 (over core), exp: 8 (over z), tp: 16 (over x, y).
Axes of the slice: x: 4, y: 4, z: 8, core: 2. Of those that a mesh axis runs over, the one named last changes fastest.
Arguments:
- residual_in: bfloat16 [2048, 8192], P(('role', 'exp', 'tp')), may hold values from -64 to 64
- context: bfloat16 [2048, 8192], P(('role', 'exp'), 'tp'), may hold values from -6 to 6
- out_weight: bfloat16 [8192, 8192], P('tp', ('role', 'exp')), may hold values from -0.0625 to 0.0625
- norm_gain: bfloat16 [8192], replicated, may hold values from 0.5 to 1.5
- router: bfloat16 [2, 4, 8192], replicated, may hold values from -0.125 to 0.125
- up_weight: bfloat16 [2, 8, 8192, 6144], P('role', 'exp', None, 'tp'), may hold values from -0.0625 to 0.0625
- down_weight: bfloat16 [2, 8, 6144, 8192], P('role', 'exp', 'tp'), may hold values from -0.109375 to 0.109375
- modality: int32 [2048], P(('role', 'exp', 'tp')), may hold values from 0 to 1
- expert: int32 [2048], P(('role', 'exp', 'tp')), may hold values from 0 to 3, as said below
Outputs:
- mixed: bfloat16 [2048, 8192], P(('role', 'exp', 'tp'))
Inputs may be any that keep to these rules, and one draw needn't show every extreme that they name: Among the 8 tokens of one device at most 2 choose one expert of one modality, and in every device's tokens some expert of some modality is chosen by exactly 2.
All inputs are finite; a program needn't handle non-finite values.
Results may differ from a plain program's by a relative error of at most 0.0052.
Values may be sent and summed in bfloat16 or wider, within the bound.
A program may use at most 128 MiB of HBM per device.

v0:
```python
import jax
import jax.numpy as jnp
from jax import lax
from jax.sharding import PartitionSpec as P

EXPERTS = 4
CAP = 2
EPSILON = 1e-05


def in_blocks(array, dim, length):
    before, after = (array.shape[:dim], array.shape[dim + 1 :])
    return jnp.moveaxis(array.reshape(*before, length, -1, *after), dim, 0)


def summed_on_arrival(array, axis, dim):
    length = lax.axis_size(axis)
    blocks = lax.all_to_all(in_blocks(array, dim, length), axis, 0, 0, tiled=True)
    return jnp.sum(blocks, axis=0)


def in_order(blocks, dim):
    blocks = jnp.moveaxis(blocks, 0, dim)
    dims = blocks.shape
    return blocks.reshape(*dims[:dim], dims[dim] * dims[dim + 1], *dims[dim + 2 :])


def joined_exchange(array, axis, axes, splits, concats):
    sizes = [lax.axis_size(a) for a in axes]
    blocks = in_blocks(array, splits[0], sizes[0])
    blocks = jnp.moveaxis(in_blocks(blocks, splits[1] + 1, sizes[1]), 0, 1)
    inside = blocks.shape[2:]
    blocks = blocks.reshape(-1, *inside)
    blocks = lax.all_to_all(blocks, axis, split_axis=0, concat_axis=0, tiled=True)
    blocks = in_order(blocks.reshape(*sizes, *inside), concats[0] + 1)
    return in_order(blocks, concats[1])


def per_device(
    residual_in, context, out_weight, norm_gain, router, up_weight, down_weight, modality, expert
):
    tok_rows, width = residual_in.shape
    head_cols = context.shape[1]
    tp_count = lax.axis_size("tp")
    group_count = lax.axis_size("role") * lax.axis_size("exp")
    exp_count = lax.axis_size("exp")
    halves = exp_count // EXPERTS
    grouped = context.reshape(tp_count, tok_rows, head_cols)
    all_rows = lax.all_gather(grouped, ("role", "exp"), axis=1, tiled=True)
    all_rows = all_rows.reshape(tp_count * group_count * tok_rows, head_cols)
    partial_cols = summed_on_arrival(
        jnp.dot(all_rows, out_weight, preferred_element_type=jnp.float32), "tp", 0
    )
    projected = lax.all_to_all(
        partial_cols.reshape(group_count, tok_rows, out_weight.shape[1]),
        ("role", "exp"),
        split_axis=0,
        concat_axis=2,
        tiled=True,
    ).reshape(tok_rows, width)
    resid = (residual_in.astype(jnp.float32) + projected).astype(jnp.bfloat16)
    resid = lax.optimization_barrier(resid)
    widened = resid.astype(jnp.float32)
    inverse_rms = lax.rsqrt(jnp.mean(widened * widened, axis=-1, keepdims=True) + EPSILON)
    normed = (widened * inverse_rms * norm_gain.astype(jnp.float32)).astype(jnp.bfloat16)
    routes = modality * EXPERTS + expert
    choices_hot = routes[:, None] == jnp.arange(2 * EXPERTS, dtype=jnp.int32)[None, :]
    hot_ints = choices_hot.astype(jnp.int32)
    earlier = jnp.cumsum(hot_ints, axis=0) - hot_ints
    position = jnp.sum(earlier * hot_ints, axis=1)
    target = routes * CAP + position
    placed = (jnp.arange(2 * EXPERTS * CAP, dtype=jnp.int32)[:, None] == target[None, :]).astype(
        jnp.bfloat16
    )
    placed = placed.reshape(2, EXPERTS, CAP, tok_rows)
    logits = lax.dot_general(
        normed,
        router.reshape(2 * EXPERTS, width),
        (((1,), (1,)), ((), ())),
        preferred_element_type=jnp.float32,
    )
    gating = jax.nn.sigmoid(jnp.sum(jnp.where(choices_hot, logits, 0.0), axis=1))
    slotted = jnp.einsum("mecq,qd->mecd", placed, normed, preferred_element_type=jnp.float32)
    slotted = slotted.astype(jnp.bfloat16)
    outgoing = jnp.broadcast_to(slotted[:, :, None], (2, EXPERTS, halves, CAP, width))
    outgoing = outgoing.reshape(2, exp_count, CAP, width)
    incoming = joined_exchange(outgoing, ("role", "exp"), ("role", "exp"), (0, 1), (0, 1))
    local_slots = incoming.reshape(2 * exp_count * CAP, width)
    up_matrix = up_weight[0, 0]
    down_matrix = down_weight[0, 0]
    up_sums = jnp.dot(
        lax.all_gather(local_slots, "tp", axis=0, tiled=True),
        up_matrix,
        preferred_element_type=jnp.float32,
    )
    hidden = jax.nn.gelu(up_sums).astype(jnp.bfloat16)
    results = lax.psum_scatter(
        jnp.dot(hidden, down_matrix, preferred_element_type=jnp.float32),
        "tp",
        scatter_dimension=0,
        tiled=True,
    )
    returned = joined_exchange(
        results.reshape(2, exp_count, CAP, width).astype(jnp.bfloat16),
        ("role", "exp"),
        ("role", "exp"),
        (0, 1),
        (0, 1),
    ).astype(jnp.float32)
    expert_out = jnp.einsum(
        "mecq,mescd->qd",
        placed.astype(jnp.float32),
        returned.reshape(2, EXPERTS, halves, CAP, width),
        precision=lax.Precision.HIGHEST,
    )
    return (widened + gating[:, None] * expert_out).astype(jnp.bfloat16)


def solution(mesh):
    in_specs = (
        P(("role", "exp", "tp"), None),
        P(("role", "exp"), "tp"),
        P("tp", ("role", "exp")),
        P(),
        P(),
        P("role", "exp", None, "tp"),
        P("role", "exp", "tp", None),
        P(("role", "exp", "tp")),
        P(("role", "exp", "tp")),
    )
    out_specs = P(("role", "exp", "tp"), None)
    return jax.shard_map(
        per_device, mesh=mesh, in_specs=in_specs, out_specs=out_specs, check_vma=False
    )
```

profile of v0, /device:TPU:32, one launch (start us, length us, event | category | flops | bytes accessed | tf_op | source)
XLA Modules:
  0.0 412.4 jit_solution(11668320973444184488)
XLA Ops:
  6.5 0.0 copy-start
  6.5 0.0 all-gather.3.cloned.1.call-start
  6.5 0.7 all-gather.3.cloned.1.call-update
  7.3 0.0 copy-start.4
  7.3 0.0 copy-start.5
  7.3 43.4 %all-gather.3.cloned.1.call-done = bf16[16,128,512]{2,1,0:T(8,128)(2,1)} async-done(((bf16[16,8,512]{2,1,0:T(8,128)(2,1)}), bf16[16,128,512]{2,1,0:T(8,128)(2,1)}) %all-gather.3.cloned.1.call-update) | async-done | bytes 2097168 | tf_op jit(solution)/shard_map/all_gather | solution.py:49
  50.6 0.0 copy-done
  50.6 4.8 %fusion.20 = f32[16,128,512]{2,1,0:T(8,128)} fusion(bf16[16,128,512]{2,1,0:T(8,128)(2,1)} %all-gather.3.cloned.1.call-done, bf16[512,512]{1,0:T(8,128)(2,1)S(1)} %copy-done), kind=kOutput, calls=%fused_computation.21 | convolution fusion | flops 1073741824 | bytes 6815744 | tf_op jit(solution)/shard_map/dot_general | solution.py:52
  55.4 0.0 copy-start.3
  55.4 0.0 copy-start.2
  55.4 7.0 %all-to-all-start = ((f32[16,128,512]{2,1,0:T(8,128)}), f32[16,128,512]{2,1,0:T(8,128)}, u32[]{:S(2)}, u32[]{:S(2)}) async-start(f32[16,128,512]{2,1,0:T(8,128)} %fusion.20), calls=%async_computation | async-start | bytes 8388608 | tf_op jit(solution)/shard_map/all_to_all | solution.py:18
  62.5 0.0 copy-done.4
  62.5 0.0 copy-done.5
  62.5 56.5 %all-to-all-done = f32[16,128,512]{2,1,0:T(8,128)} async-done(((f32[16,128,512]{2,1,0:T(8,128)}), f32[16,128,512]{2,1,0:T(8,128)}, u32[]{:S(2)}, u32[]{:S(2)}) %all-to-all-start) | async-done | bytes 4194336 | tf_op jit(solution)/shard_map/all_to_all | solution.py:18
  119.0 3.3 reduce_sum.45
  122.3 4.9 %all-to-all-start.1 = ((f32[16,8,512]{2,1,0:T(8,128)}), f32[16,8,512]{2,1,0:T(8,128)S(1)}, u32[]{:S(2)}, u32[]{:S(2)}) async-start(f32[16,8,512]{2,1,0:T(8,128)} %bitcast.2), calls=%async_computation.1 | async-start | bytes 524288 | tf_op jit(solution)/shard_map/all_to_all | solution.py:54
  127.2 0.0 all-gather.5.cloned.1.call-start
  127.2 0.0 copy-done.3
  127.2 0.2 reduce_window_sum.11
  127.4 10.6 %all-to-all-done.1 = f32[16,8,512]{2,1,0:T(8,128)S(1)} async-done(((f32[16,8,512]{2,1,0:T(8,128)}), f32[16,8,512]{2,1,0:T(8,128)S(1)}, u32[]{:S(2)}, u32[]{:S(2)}) %all-to-all-start.1) | async-done | bytes 262176 | tf_op jit(solution)/shard_map/all_to_all | solution.py:54
  138.1 0.0 copy-done.2
  138.1 0.2 fusion.23
  138.3 0.3 convolution_convert_fusion
  138.6 0.3 copy.13
  138.9 0.4 broadcast_in_dim.6
  139.3 19.8 %all_to_all.30 = bf16[16,1,1,2,8192]{4,3,2,1,0:T(2,128)(2,1)S(1)} all-to-all(bf16[16,1,1,2,8192]{4,3,2,1,0:T(2,128)(2,1)S(1)} %bitcast.64), channel_id=1, replica_groups=mesh['role'=2,'exp'=8,'tp'=16] {'role','exp'}, dimensions={0} | all-to-all | bytes 1048576 | tf_op jit(solution)/shard_map/all_to_all | solution.py:34
  159.1 1.0 reshape_reshape.3
  160.1 0.0 all-gather.5.cloned.1.call-update
  160.1 0.0 reduce-scatter.2.cloned.1.call-start
  160.2 80.9 %all-gather.5.cloned.1.call-done = bf16[512,8192]{1,0:T(8,128)(2,1)} async-done(((bf16[32,8192]{1,0:T(8,128)(2,1)}), bf16[512,8192]{1,0:T(8,128)(2,1)}) %all-gather.5.cloned.1.call-update) | async-done | bytes 8388624 | tf_op jit(solution)/shard_map/all_gather | solution.py:92
  241.0 9.8 %fusion.17 = bf16[512,384]{1,0:T(8,128)(2,1)S(1)} fusion(bf16[512,8192]{1,0:T(8,128)(2,1)} %all-gather.5.cloned.1.call-done, bf16[1,1,8192,384]{3,2,1,0:T(8,128)(2,1)} %param.14), kind=kOutput, calls=%fused_computation.20 | convolution fusion | flops 3222994944 | bytes 15073280 | tf_op jit(solution)/shard_map/dot_general | solution.py:91
  250.8 10.9 %fusion.3 = f32[512,8192]{1,0:T(8,128)} fusion(bf16[512,384]{1,0:T(8,128)(2,1)S(1)} %fusion.17, bf16[1,1,384,8192]{3,2,1,0:T(8,128)(2,1)} %param.15), kind=kOutput, calls=%fused_computation.5 | convolution fusion | flops 3221225472 | bytes 23461888 | tf_op jit(solution)/shard_map/dot_general | solution.py:98
  261.7 0.0 copy-start.1
  261.7 0.0 reduce-scatter.2.cloned.1.call-update
  261.7 115.6 %reduce-scatter.2.cloned.1.call-done = f32[32,8192]{1,0:T(8,128)} async-done(((f32[512,8192]{1,0:T(8,128)}), f32[32,8192]{1,0:T(8,128)}) %reduce-scatter.2.cloned.1.call-update) | async-done | bytes 1048592 | tf_op jit(solution)/shard_map/reduce_scatter | solution.py:97
  377.4 1.3 convert_element_type.70
  378.7 1.1 convert_element_type.71
  379.8 7.6 %all-to-all-start.3 = ((bf16[16,1,1,2,8192]{4,3,2,1,0:T(2,128)(2,1)}), bf16[16,1,1,2,8192]{4,3,2,1,0:T(2,128)(2,1)S(1)}, u32[]{:S(2)}, u32[]{:S(2)}) async-start(bf16[16,1,1,2,8192]{4,3,2,1,0:T(2,128)(2,1)} %bitcast.15), calls=%async_computation.4 | async-start | bytes 1048576 | tf_op jit(solution)/shard_map/all_to_all | solution.py:34
  387.4 0.0 copy-done.1
  387.4 0.3 fusion.7
  387.7 16.0 %all-to-all-done.3 = bf16[16,1,1,2,8192]{4,3,2,1,0:T(2,128)(2,1)S(1)} async-done(((bf16[16,1,1,2,8192]{4,3,2,1,0:T(2,128)(2,1)}), bf16[16,1,1,2,8192]{4,3,2,1,0:T(2,128)(2,1)S(1)}, u32[]{:S(2)}, u32[]{:S(2)}) %all-to-all-start.3) | async-done | bytes 524320 | tf_op jit(solution)/shard_map/all_to_all | solution.py:34
  403.7 0.6 convert_reduce_fusion
  404.3 1.6 fusion.2
  (10 shorter events, 0.1 us)
Async XLA Ops:
  6.5 44.1 %copy-start = (bf16[512,512]{1,0:T(8,128)(2,1)S(1)}, bf16[512,512]{1,0:T(8,128)(2,1)}, u32[]{:S(2)}) copy-start(bf16[512,512]{1,0:T(8,128)(2,1)} %param.11) | copy-start | bytes 1572868
  6.5 44.1 %all-gather.3.cloned.1.call-start = ((), (), s32[]{:S(2)}) async-start(), calls=%async_computation.5 | async-start | bytes 2228224 | tf_op jit(solution)/shard_map/all_gather | solution.py:49
  7.3 55.2 %copy-start.4 = (s32[8]{0:T(128)S(1)}, s32[8]{0:T(128)}, u32[]{:S(2)}) copy-start(s32[8]{0:T(128)} %param.17) | copy-start | bytes 100
  7.3 55.2 %copy-start.5 = (s32[8]{0:T(128)S(1)}, s32[8]{0:T(128)}, u32[]{:S(2)}) copy-start(s32[8]{0:T(128)} %param.16) | copy-start | bytes 100
  55.4 71.8 %copy-start.3 = (bf16[8192]{0:T(1024)(128)(2,1)S(1)}, bf16[8192]{0:T(1024)(128)(2,1)}, u32[]{:S(2)}) copy-start(bf16[8192]{0:T(1024)(128)(2,1)} %param.12) | copy-start | bytes 49156
  55.4 82.6 %copy-start.2 = (bf16[8,8192]{1,0:T(8,128)(2,1)S(1)}, bf16[8,8192]{1,0:T(8,128)(2,1)}, u32[]{:S(2)}) copy-start(bf16[8,8192]{1,0:T(8,128)(2,1)} %param.9) | copy-start | bytes 393220
  55.4 63.5 %all-to-all-start = ((f32[16,128,512]{2,1,0:T(8,128)}), f32[16,128,512]{2,1,0:T(8,128)}, u32[]{:S(2)}, u32[]{:S(2)}) async-start(f32[16,128,512]{2,1,0:T(8,128)} %fusion.20), calls=%async_computation | async-start | bytes 8388608 | tf_op jit(solution)/shard_map/all_to_all | solution.py:18
  122.3 15.8 %all-to-all-start.1 = ((f32[16,8,512]{2,1,0:T(8,128)}), f32[16,8,512]{2,1,0:T(8,128)S(1)}, u32[]{:S(2)}, u32[]{:S(2)}) async-start(f32[16,8,512]{2,1,0:T(8,128)} %bitcast.2), calls=%async_computation.1 | async-start | bytes 524288 | tf_op jit(solution)/shard_map/all_to_all | solution.py:54
  127.2 113.9 %all-gather.5.cloned.1.call-start = ((), (), s32[]{:S(2)}) async-start(), calls=%async_computation.6 | async-start | bytes 8912896 | tf_op jit(solution)/shard_map/all_gather | solution.py:92
  160.1 217.3 %reduce-scatter.2.cloned.1.call-start = ((), (), s32[]{:S(2)}) async-start(), calls=%async_computation.7 | async-start | bytes 17825792 | tf_op jit(solution)/shard_map/reduce_scatter | solution.py:97
  261.7 125.7 %copy-start.1 = (bf16[2,4,8192]{2,1,0:T(4,128)(2,1)S(1)}, bf16[2,4,8192]{2,1,0:T(4,128)(2,1)}, u32[]{:S(2)}) copy-start(bf16[2,4,8192]{2,1,0:T(4,128)(2,1)} %param.13) | copy-start | bytes 393220
  379.8 23.9 %all-to-all-start.3 = ((bf16[16,1,1,2,8192]{4,3,2,1,0:T(2,128)(2,1)}), bf16[16,1,1,2,8192]{4,3,2,1,0:T(2,128)(2,1)S(1)}, u32[]{:S(2)}, u32[]{:S(2)}) async-start(bf16[16,1,1,2,8192]{4,3,2,1,0:T(2,128)(2,1)} %bitcast.15), calls=%async_computation.4 | async-start | bytes 1048576 | tf_op jit(solution)/shard_map/all_to_all | solution.py:34
Sparse Core Ops, SparseCore 0:
  9.2 41.4 all-gather.2
  160.3 80.7 all-gather.4
  261.9 115.4 reduce-scatter.1
where the time goes:
time: 413 us; the launch traced here: 412 us
  waiting for transfers between devices  324 us (78%)
  matrix products  27.6 us (7%)
  blocking collectives  19.8 us (5%)
  starting transfers between devices  19.6 us (5%)
  between operations  13.2 us (3%)
  other arithmetic  5.66 us (1%)
    reduce_scatter x1, waiting for transfers between devices, per_device(): lax.psum_scatter(jnp.dot(hidden, down_matrix, preferred_element_type=jnp....  116 us
    all_gather x1, waiting for transfers between devices, per_device(): lax.all_gather(local_slots, 'tp', axis=0, tiled=True)  80.9 us
    all_to_all x1, waiting for transfers between devices, summed_on_arrival(): lax.all_to_all(in_blocks(array, dim, length), axis, 0, 0, tiled=True)  56.5 us
    all_gather x1, waiting for transfers between devices, per_device(): all_rows = lax.all_gather(grouped, ('role', 'exp'), axis=1, tiled=True)  43.4 us
    all_to_all x1, blocking collectives, joined_exchange(): lax.all_to_all(blocks, axis, split_axis=0, concat_axis=0, tiled=True)  19.8 us
    all_to_all x1, waiting for transfers between devices, joined_exchange(): lax.all_to_all(blocks, axis, split_axis=0, concat_axis=0, tiled=True)  16 us
    dot_general x1, matrix products, per_device(): jnp.dot(hidden, down_matrix, preferred_element_type=jnp.float32)  10.9 us
    all_to_all x1, waiting for transfers between devices, per_device(): lax.all_to_all(partial_cols.reshape(group_count, tok_rows, out_weight.sha...  10.6 us
  transfers between devices with their start and end apart: 6, of which 6 were waited for; matrix products, arithmetic and copies ran while one was open for 0% of the time, Pallas kernels for 0%

commit v1 on v0

--- a/solution.py
+++ b/solution.py
@@ -89,7 +89,9 @@
     up_matrix = up_weight[0, 0]
     down_matrix = down_weight[0, 0]
     up_sums = jnp.dot(
-        lax.all_gather(local_slots, "tp", axis=0, tiled=True),
+        jnp.concatenate(
+            lax.all_to_all(jnp.stack([local_slots] * lax.axis_size("tp")), "tp", 0, 0), axis=0
+        ),
         up_matrix,
         preferred_element_type=jnp.float32,
     )

time: 413 us -> 434 us (1.051)
  blocking collectives: 19.8 us -> 129 us
  waiting for transfers between devices: 324 us -> 241 us
  matrix products: 27.6 us -> 22.6 us
    all_to_all x0 -> x1, blocking collectives: none -> 109 us  [per_device(): lax.all_to_all(jnp.stack([local_slots] * lax.axis_size('tp')), 'tp', 0, 0)]
    all_gather x1 -> x0, waiting for transfers between devices: 80.9 us -> none  [per_device(): lax.all_gather(local_slots, 'tp', axis=0, tiled=True)]
  transfers between devices with their start and end apart: 6 -> 5, of which waited for: 6 -> 5; matrix products, arithmetic and copies ran while one was open for 0% -> 0% of each run, Pallas kernels for 0% -> 0%
where the time goes in v1:
time: 434 us
  waiting for transfers between devices  241 us (56%)
  blocking collectives  129 us (30%)
  matrix products  22.6 us (5%)
  starting transfers between devices  19.4 us (4%)
  between operations  13.6 us (3%)
  other arithmetic  5.65 us (1%)
    reduce_scatter x1, waiting for transfers between devices, per_device(): lax.psum_scatter(jnp.dot(hidden, down_matrix, preferred_element_type=jnp....  114 us
    all_to_all x1, blocking collectives, per_device(): lax.all_to_all(jnp.stack([local_slots] * lax.axis_size('tp')), 'tp', 0, 0)  109 us
    all_to_all x1, waiting for transfers between devices, summed_on_arrival(): lax.all_to_all(in_blocks(array, dim, length), axis, 0, 0, tiled=True)  56.5 us
    all_gather x1, waiting for transfers between devices, per_device(): all_rows = lax.all_gather(grouped, ('role', 'exp'), axis=1, tiled=True)  43.4 us
    all_to_all x1, blocking collectives, joined_exchange(): lax.all_to_all(blocks, axis, split_axis=0, concat_axis=0, tiled=True)  19.8 us
    all_to_all x1, waiting for transfers between devices, joined_exchange(): lax.all_to_all(blocks, axis, split_axis=0, concat_axis=0, tiled=True)  16 us
    all_to_all x1, waiting for transfers between devices, per_device(): lax.all_to_all(partial_cols.reshape(group_count, tok_rows, out_weight.sha...  10.6 us
  transfers between devices with their start and end apart: 5, of which 5 were waited for; matrix products, arithmetic and copies ran while one was open for 0% of the time, Pallas kernels for 0%

profile of v1, /device:TPU:32, one launch (start us, length us, event | category | flops | bytes accessed | tf_op | source)
XLA Modules:
  0.0 433.6 jit_solution(5413107088751852799)
XLA Ops:
  6.5 0.0 copy-start
  6.5 0.0 all-gather.2.cloned.1.call-start
  6.5 0.7 all-gather.2.cloned.1.call-update
  7.3 0.0 copy-start.4
  7.3 0.0 copy-start.5
  7.3 43.4 %all-gather.2.cloned.1.call-done = bf16[16,128,512]{2,1,0:T(8,128)(2,1)} async-done(((bf16[16,8,512]{2,1,0:T(8,128)(2,1)}), bf16[16,128,512]{2,1,0:T(8,128)(2,1)}) %all-gather.2.cloned.1.call-update) | async-done | bytes 2097168 | tf_op jit(solution)/shard_map/all_gather | solution.py:49
  50.6 0.0 copy-done
  50.6 4.8 %fusion.20 = f32[16,128,512]{2,1,0:T(8,128)} fusion(bf16[16,128,512]{2,1,0:T(8,128)(2,1)} %all-gather.2.cloned.1.call-done, bf16[512,512]{1,0:T(8,128)(2,1)S(1)} %copy-done), kind=kOutput, calls=%fused_computation.21 | convolution fusion | flops 1073741824 | bytes 6815744 | tf_op jit(solution)/shard_map/dot_general | solution.py:52
  55.4 0.0 copy-start.3
  55.4 0.0 copy-start.2
  55.4 7.0 %all-to-all-start = ((f32[16,128,512]{2,1,0:T(8,128)}), f32[16,128,512]{2,1,0:T(8,128)}, u32[]{:S(2)}, u32[]{:S(2)}) async-start(f32[16,128,512]{2,1,0:T(8,128)} %fusion.20), calls=%async_computation | async-start | bytes 8388608 | tf_op jit(solution)/shard_map/all_to_all | solution.py:18
  62.4 0.0 copy-done.4
  62.5 0.0 copy-done.5
  62.5 56.5 %all-to-all-done = f32[16,128,512]{2,1,0:T(8,128)} async-done(((f32[16,128,512]{2,1,0:T(8,128)}), f32[16,128,512]{2,1,0:T(8,128)}, u32[]{:S(2)}, u32[]{:S(2)}) %all-to-all-start) | async-done | bytes 4194336 | tf_op jit(solution)/shard_map/all_to_all | solution.py:18
  119.0 3.3 reduce_sum.45
  122.3 4.9 %all-to-all-start.1 = ((f32[16,8,512]{2,1,0:T(8,128)}), f32[16,8,512]{2,1,0:T(8,128)S(1)}, u32[]{:S(2)}, u32[]{:S(2)}) async-start(f32[16,8,512]{2,1,0:T(8,128)} %bitcast.2), calls=%async_computation.1 | async-start | bytes 524288 | tf_op jit(solution)/shard_map/all_to_all | solution.py:54
  127.2 0.0 reduce-scatter.2.cloned.1.call-start
  127.2 0.0 copy-done.3
  127.2 0.2 reduce_window_sum.11
  127.4 10.6 %all-to-all-done.1 = f32[16,8,512]{2,1,0:T(8,128)S(1)} async-done(((f32[16,8,512]{2,1,0:T(8,128)}), f32[16,8,512]{2,1,0:T(8,128)S(1)}, u32[]{:S(2)}, u32[]{:S(2)}) %all-to-all-start.1) | async-done | bytes 262176 | tf_op jit(solution)/shard_map/all_to_all | solution.py:54
  138.1 0.0 copy-done.2
  138.1 0.2 fusion.23
  138.3 0.3 convolution_convert_fusion
  138.6 0.3 copy.13
  138.9 0.4 broadcast_in_dim.6
  139.3 19.8 %all_to_all.35 = bf16[16,1,1,2,8192]{4,3,2,1,0:T(2,128)(2,1)S(1)} all-to-all(bf16[16,1,1,2,8192]{4,3,2,1,0:T(2,128)(2,1)S(1)} %bitcast.68), channel_id=1, replica_groups=mesh['role'=2,'exp'=8,'tp'=16] {'role','exp'}, dimensions={0} | all-to-all | bytes 1048576 | tf_op jit(solution)/shard_map/all_to_all | solution.py:34
  159.1 0.2 stack_reshape_reshape.2
  159.3 1.0 stack.3
  160.3 0.0 slice-start
  160.3 108.8 %all_to_all.36 = bf16[16,32,8192]{2,1,0:T(8,128)(2,1)S(1)} all-to-all(bf16[16,32,8192]{2,1,0:T(8,128)(2,1)S(1)} %stack.3), channel_id=1, replica_groups=mesh['role'=2,'exp'=8,'tp'=16] {'tp'}, dimensions={0} | all-to-all | bytes 16777216 | tf_op jit(solution)/shard_map/all_to_all | solution.py:93
  269.1 0.0 slice-start.1
  269.1 7.5 %fusion.17 = bf16[512,384]{1,0:T(8,128)(2,1)S(1)} fusion(bf16[512,8192]{1,0:T(8,128)(2,1)S(1)} %bitcast.64, bf16[1,1,8192,384]{3,2,1,0:T(8,128)(2,1)} %param.14), kind=kOutput, calls=%fused_computation.20 | convolution fusion | flops 3222994944 | bytes 15073280 | tf_op jit(solution)/shard_map/dot_general | solution.py:91
  276.6 0.0 slice-done
  276.7 0.0 slice-done.1
  276.7 8.1 %fusion.3 = f32[512,8192]{1,0:T(8,128)} fusion(bf16[512,384]{1,0:T(8,128)(2,1)S(1)} %fusion.17, bf16[1,1,384,8192]{3,2,1,0:T(8,128)(2,1)S(1)} %bitcast.66), kind=kOutput, calls=%fused_computation.5 | convolution fusion | flops 3221225472 | bytes 23461888 | tf_op jit(solution)/shard_map/dot_general | solution.py:100
  284.7 0.0 copy-start.1
  284.7 0.0 reduce-scatter.2.cloned.1.call-update
  284.8 113.6 %reduce-scatter.2.cloned.1.call-done = f32[32,8192]{1,0:T(8,128)} async-done(((f32[512,8192]{1,0:T(8,128)}), f32[32,8192]{1,0:T(8,128)}) %reduce-scatter.2.cloned.1.call-update) | async-done | bytes 1048592 | tf_op jit(solution)/shard_map/reduce_scatter | solution.py:99
  398.3 1.3 convert_element_type.70
  399.6 1.1 convert_element_type.71
  400.7 7.5 %all-to-all-start.4 = ((bf16[16,1,1,2,8192]{4,3,2,1,0:T(2,128)(2,1)}), bf16[16,1,1,2,8192]{4,3,2,1,0:T(2,128)(2,1)S(1)}, u32[]{:S(2)}, u32[]{:S(2)}) async-start(bf16[16,1,1,2,8192]{4,3,2,1,0:T(2,128)(2,1)} %bitcast.16), calls=%async_computation.5 | async-start | bytes 1048576 | tf_op jit(solution)/shard_map/all_to_all | solution.py:34
  408.2 0.0 copy-done.1
  408.3 0.3 fusion.7
  408.6 16.0 %all-to-all-done.4 = bf16[16,1,1,2,8192]{4,3,2,1,0:T(2,128)(2,1)S(1)} async-done(((bf16[16,1,1,2,8192]{4,3,2,1,0:T(2,128)(2,1)}), bf16[16,1,1,2,8192]{4,3,2,1,0:T(2,128)(2,1)S(1)}, u32[]{:S(2)}, u32[]{:S(2)}) %all-to-all-start.4) | async-done | bytes 524320 | tf_op jit(solution)/shard_map/all_to_all | solution.py:34
  424.6 0.6 convert_reduce_fusion
  425.2 1.6 fusion.2
  (11 shorter events, 0.1 us)
Async XLA Ops:
  6.5 44.1 %copy-start = (bf16[512,512]{1,0:T(8,128)(2,1)S(1)}, bf16[512,512]{1,0:T(8,128)(2,1)}, u32[]{:S(2)}) copy-start(bf16[512,512]{1,0:T(8,128)(2,1)} %param.11) | copy-start | bytes 1572868
  6.5 44.1 %all-gather.2.cloned.1.call-start = ((), (), s32[]{:S(2)}) async-start(), calls=%async_computation.6 | async-start | bytes 2228224 | tf_op jit(solution)/shard_map/all_gather | solution.py:49
  7.3 55.2 %copy-start.4 = (s32[8]{0:T(128)S(1)}, s32[8]{0:T(128)}, u32[]{:S(2)}) copy-start(s32[8]{0:T(128)} %param.17) | copy-start | bytes 100
  7.3 55.2 %copy-start.5 = (s32[8]{0:T(128)S(1)}, s32[8]{0:T(128)}, u32[]{:S(2)}) copy-start(s32[8]{0:T(128)} %param.16) | copy-start | bytes 100
  55.4 71.8 %copy-start.3 = (bf16[8192]{0:T(1024)(128)(2,1)S(1)}, bf16[8192]{0:T(1024)(128)(2,1)}, u32[]{:S(2)}) copy-start(bf16[8192]{0:T(1024)(128)(2,1)} %param.12) | copy-start | bytes 49156
  55.4 82.6 %copy-start.2 = (bf16[8,8192]{1,0:T(8,128)(2,1)S(1)}, bf16[8,8192]{1,0:T(8,128)(2,1)}, u32[]{:S(2)}) copy-start(bf16[8,8192]{1,0:T(8,128)(2,1)} %param.9) | copy-start | bytes 393220
  55.4 63.5 %all-to-all-start = ((f32[16,128,512]{2,1,0:T(8,128)}), f32[16,128,512]{2,1,0:T(8,128)}, u32[]{:S(2)}, u32[]{:S(2)}) async-start(f32[16,128,512]{2,1,0:T(8,128)} %fusion.20), calls=%async_computation | async-start | bytes 8388608 | tf_op jit(solution)/shard_map/all_to_all | solution.py:18
  122.3 15.8 %all-to-all-start.1 = ((f32[16,8,512]{2,1,0:T(8,128)}), f32[16,8,512]{2,1,0:T(8,128)S(1)}, u32[]{:S(2)}, u32[]{:S(2)}) async-start(f32[16,8,512]{2,1,0:T(8,128)} %bitcast.2), calls=%async_computation.1 | async-start | bytes 524288 | tf_op jit(solution)/shard_map/all_to_all | solution.py:54
  127.2 271.2 %reduce-scatter.2.cloned.1.call-start = ((), (), s32[]{:S(2)}) async-start(), calls=%async_computation.7 | async-start | bytes 17825792 | tf_op jit(solution)/shard_map/reduce_scatter | solution.py:99
  160.3 116.3 %slice-start = ((s8[6291456]{0:T(1024)(128)(4,1)}), s8[4194304]{0:T(1024)(128)(4,1)S(1)}, s32[]{:S(2)}) async-start(s8[6291456]{0:T(1024)(128)(4,1)} %bitcast.65), calls=%async_computation.8 | async-start | bytes 8388608
  269.1 7.6 %slice-start.1 = ((s8[6291456]{0:T(1024)(128)(4,1)}), s8[2097152]{0:T(1024)(128)(4,1)S(1)}, s32[]{:S(2)}) async-start(s8[6291456]{0:T(1024)(128)(4,1)} %bitcast.65), calls=%async_computation.9 | async-start | bytes 4194304
  284.7 123.5 %copy-start.1 = (bf16[2,4,8192]{2,1,0:T(4,128)(2,1)S(1)}, bf16[2,4,8192]{2,1,0:T(4,128)(2,1)}, u32[]{:S(2)}) copy-start(bf16[2,4,8192]{2,1,0:T(4,128)(2,1)} %param.13) | copy-start | bytes 393220
  400.7 23.8 %all-to-all-start.4 = ((bf16[16,1,1,2,8192]{4,3,2,1,0:T(2,128)(2,1)}), bf16[16,1,1,2,8192]{4,3,2,1,0:T(2,128)(2,1)S(1)}, u32[]{:S(2)}, u32[]{:S(2)}) async-start(bf16[16,1,1,2,8192]{4,3,2,1,0:T(2,128)(2,1)} %bitcast.16), calls=%async_computation.5 | async-start | bytes 1048576 | tf_op jit(solution)/shard_map/all_to_all | solution.py:34
Sparse Core Ops, SparseCore 0:
  9.2 41.4 all-gather.1
  284.9 113.4 reduce-scatter.1
